TPU v7x, 256 devices: a whole 4x4x8 slice. The times are simulated.
256 devices in a mesh: dp: 8 (over x_lo, y), owner: 8 (over z), context: 4 (over x_hi, core).
Axes of the slice: x: 4 (x_hi: 2, x_lo: 2; x = x_hi * 2 + x_lo), y: 4, z: 8, core: 2. Of those that a mesh axis runs over, the one named last changes fastest.
Arguments:
- grad_partials: bfloat16 [32, 1536, 64, 192], P(('dp', 'context'), None, 'owner')
- assignment: int32 [64, 1], replicated, may hold values from 0 to 7; in each aligned block of 8 rows (0 to 7, 8 to 15, ...) at most 2 rows name the same one
- momentum: float32 [128, 1536, 192], P('owner', ('dp', 'context')), may hold values from -6 to 6
- q_weight: float32 [128, 1536, 192], P('owner', ('dp', 'context')), may hold values from -1.2 to 1.2
- k_weight: float32 [64, 512, 128], P('owner', ('dp', 'context')), may hold values from -6 to 6
- max_logits: float32 [4, 64], P('context'), may hold values from 20 to 400
Outputs:
- momentum_out: float32 [128, 1536, 192], P('owner', ('dp', 'context'))
- q_weight_out: float32 [128, 1536, 192], P('owner', ('dp', 'context'))
- k_weight_out: float32 [64, 512, 128], P('owner', ('dp', 'context'))
Inputs may be any that keep to these rules, and one draw needn't show every extreme that they name: `assignment`: in each aligned block of 8 heads no owner index is named more than 2 times, and some owner index exactly 2 times.
All inputs are finite; a program needn't handle non-finite values.
Results may differ from a plain program's by a relative error of at most 0.0007.
Values may be sent and summed in bfloat16 or wider, within the bound.
A program may use at most 128 MiB of HBM per device.

v0:
```python
import math
import jax
import jax.numpy as jnp
from jax import lax
from jax.sharding import PartitionSpec as P

QR = 1536
QK = 192
ITERS = 2
MOMENTUM_RATE = 0.95
WEIGHT_KEEP = 0.98
LOGIT_CAP = 100.0
QUINTIC_A = 3.4445
QUINTIC_B = -4.775
QUINTIC_C = 2.0315


def routing(assignment, heads_own, per_source):
    target = assignment[:, 0]
    head_index = jnp.arange(target.shape[0], dtype=jnp.int32)
    source_block = head_index // heads_own
    earlier = (
        (source_block[None, :] == source_block[:, None])
        & (head_index[None, :] < head_index[:, None])
        & (target[None, :] == target[:, None])
    )
    position = jnp.sum(earlier.astype(jnp.int32), axis=1)
    return (target, position, source_block * per_source + position)


def refresh(weight, orthogonal, gamma, kn_count):
    step_size = 0.04 * math.sqrt(max(QR, QK))
    column_index = jnp.arange(weight.shape[2])
    column_scale = jnp.where(
        column_index[None, :] < kn_count, jnp.sqrt(gamma)[:, None], gamma[:, None]
    )
    return (WEIGHT_KEEP * weight - step_size * orthogonal.astype(jnp.float32)) * column_scale[
        :, None, :
    ]


def quintic(whole):
    for step in range(ITERS):
        gram_matrix = jnp.einsum("nrk,nrl->nkl", whole, whole, preferred_element_type=jnp.float32)
        polynomial = (
            QUINTIC_B * gram_matrix
            + QUINTIC_C
            * jnp.einsum("nkl,nlm->nkm", gram_matrix, gram_matrix, precision=lax.Precision.HIGHEST)
        ).astype(jnp.bfloat16)
        whole = (
            QUINTIC_A * whole.astype(jnp.float32)
            + jnp.einsum("nrk,nkl->nrl", whole, polynomial, preferred_element_type=jnp.float32)
        ).astype(jnp.bfloat16)
    return whole


def orthogonalize(matrix):
    square_sum = lax.psum(jnp.sum(matrix * matrix, axis=(1, 2)), ("dp", "context"))
    iterate = (matrix / (jnp.sqrt(square_sum) + 1e-07)[:, None, None]).astype(jnp.bfloat16)
    row_count = matrix.shape[1]
    gathered = lax.all_gather(iterate, ("dp", "context"), axis=1, tiled=True)
    gathered = quintic(gathered)
    return lax.dynamic_slice_in_dim(
        gathered, lax.axis_index(("dp", "context")) * row_count, row_count, 1
    )


def body(grad_partials, assignment, momentum, q_weight, k_weight, max_logits):
    heads_own = grad_partials.shape[2]
    slots_own = momentum.shape[0]
    kn_count = k_weight.shape[2]
    per_source = slots_own // lax.axis_size("owner")
    my_owner = lax.axis_index("owner")
    target, position, local_slot = routing(assignment, heads_own, per_source)
    peak_logit = lax.pmax(max_logits[0], "context")
    gamma = jnp.minimum(1.0, LOGIT_CAP / peak_logit)
    partial_value = grad_partials[0]
    grad_rows = lax.psum_scatter(
        partial_value.astype(jnp.float32), ("dp", "context"), scatter_dimension=0, tiled=True
    )
    home_target = lax.dynamic_slice_in_dim(target, my_owner * heads_own, heads_own)
    home_position = lax.dynamic_slice_in_dim(position, my_owner * heads_own, heads_own)
    send_index = home_target * per_source + home_position
    slot_index = jnp.arange(slots_own, dtype=jnp.int32)
    sender = (slot_index[:, None] == send_index[None, :]).astype(jnp.float32)
    owned_mask = (
        (target[None, :] == my_owner) & (local_slot[None, :] == slot_index[:, None])
    ).astype(jnp.float32)
    occupied = (jnp.sum(owned_mask, axis=1) > 0.5)[:, None, None]
    home_gamma = lax.dynamic_slice_in_dim(gamma, my_owner * heads_own, heads_own)
    outgoing = jnp.einsum("qi,rik->qrk", sender, grad_rows, precision=lax.Precision.HIGHEST)
    arrived = lax.all_to_all(outgoing, "owner", split_axis=0, concat_axis=0, tiled=True)
    refreshed = jnp.where(occupied, MOMENTUM_RATE * momentum + arrived, momentum)
    orthogonal = orthogonalize(refreshed)
    slot_gamma = jnp.sum(owned_mask * gamma[None, :], axis=1)
    slot_gamma = jnp.where(occupied[:, 0, 0], slot_gamma, 1.0)
    q_weight_out = jnp.where(
        occupied, refresh(q_weight, orthogonal, slot_gamma, kn_count), q_weight
    )
    k_weight_out = k_weight * jnp.sqrt(home_gamma)[:, None, None]
    return (refreshed, q_weight_out, k_weight_out)


def solution(mesh):
    placed = (
        P(("dp", "context"), None, "owner", None),
        P(),
        P("owner", ("dp", "context"), None),
        P("owner", ("dp", "context"), None),
        P("owner", ("dp", "context"), None),
        P("context", None),
    )
    return jax.shard_map(
        body,
        mesh=mesh,
        in_specs=placed,
        out_specs=(
            P("owner", ("dp", "context"), None),
            P("owner", ("dp", "context"), None),
            P("owner", ("dp", "context"), None),
        ),
        check_vma=False,
    )
```

profile of v0, /device:TPU:1, one launch (start us, length us, event | category | flops | bytes accessed | tf_op | source)
XLA Modules:
  0.0 456.4 jit_solution(1013946448971146130)
XLA Ops:
  7.2 0.0 reduce-scatter.2.cloned.1.call-start
  7.2 9.2 %copy.57 = bf16[1,1536,8,192]{3,2,1,0:T(8,128)(2,1)} copy(bf16[1,1536,8,192]{1,3,2,0:T(8,128)(2,1)} %param.6) | data formatting | bytes 9437184 | tf_op args[0]
  16.4 7.5 %bitcast_convert_fusion = f32[1536,8,192]{2,1,0:T(8,128)} fusion(bf16[1,1536,8,192]{3,2,1,0:T(8,128)(2,1)} %copy.57), kind=kLoop, calls=%fused_computation.4 | loop fusion | flops 2359296 | bytes 14155776 | tf_op jit(solution)/shard_map/convert_element_type | solution.py:79
  23.8 0.0 copy-start.4
  23.8 0.0 reduce-scatter.2.cloned.1.call-update
  23.9 0.0 copy-start.5
  23.9 0.0 copy-start.1
  23.9 0.6 copy-done.4
  24.5 0.2 convert_reduce_fusion
  24.7 0.1 fusion.13
  24.7 175.2 %reduce-scatter.2.cloned.1.call-done = f32[48,8,192]{2,1,0:T(8,128)} async-done(((f32[1536,8,192]{2,1,0:T(8,128)}), f32[48,8,192]{2,1,0:T(8,128)}) %reduce-scatter.2.cloned.1.call-update) | async-done | bytes 294928 | tf_op jit(solution)/shard_map/reduce_scatter | solution.py:78
  199.9 1.6 fusion.8
  201.5 1.3 copy.58
  202.9 0.0 copy-start.3
  202.9 8.6 %all-to-all-start = ((f32[16,48,192]{2,1,0:T(8,128)}), f32[16,48,192]{2,1,0:T(8,128)S(1)}, u32[]{:S(2)}, u32[]{:S(2)}) async-start(f32[16,48,192]{2,1,0:T(8,128)} %copy.58), calls=%async_computation.1 | async-start | bytes 1572864 | tf_op jit(solution)/shard_map/all_to_all | solution.py:92
  211.5 0.0 all-gather.2.cloned.1.call-start
  211.5 0.0 copy-done.5
  211.5 10.9 %pmax.7 = f32[64]{0:T(128)S(1)} all-reduce(f32[64]{0:T(128)S(1)} %bitcast.24), channel_id=1, replica_groups=mesh['dp'=8,'owner'=8,'context'=4] {'context'}, use_global_device_ids=true, to_apply=%region_5.6 | all-reduce | flops 64 | bytes 512 | tf_op jit(solution)/shard_map/pmax | solution.py:75
  222.4 0.1 select_reduce_fusion
  222.5 8.9 %all-to-all-done = f32[16,48,192]{2,1,0:T(8,128)S(1)} async-done(((f32[16,48,192]{2,1,0:T(8,128)}), f32[16,48,192]{2,1,0:T(8,128)S(1)}, u32[]{:S(2)}, u32[]{:S(2)}) %all-to-all-start) | async-done | bytes 589856 | tf_op jit(solution)/shard_map/all_to_all | solution.py:92
  231.4 0.0 copy-done.1
  231.4 0.3 multiply_reduce_fusion
  231.7 0.0 copy-start
  231.8 66.2 %psum.7 = f32[16]{0:T(128)S(1)} all-reduce(f32[16]{0:T(128)S(1)} %get-tuple-element.16), channel_id=1, replica_groups=mesh['dp'=8,'owner'=8,'context'=4] {'dp','context'}, use_global_device_ids=true, to_apply=%region_4.5 | all-reduce | flops 16 | bytes 128 | tf_op jit(solution)/shard_map/psum | solution.py:58
  297.9 0.1 divide_convert_fusion
  298.1 0.9 copy.59
  298.9 0.0 all-gather.2.cloned.1.call-update
  299.0 0.1 dynamic-slice_sqrt_fusion
  299.1 0.1 broadcast_select_fusion
  299.1 0.0 copy-done.3
  299.1 0.7 broadcast_multiply_fusion
  299.9 73.1 %all-gather.2.cloned.1.call-done = bf16[16,1536,192]{2,0,1:T(8,128)(2,1)} async-done(((bf16[16,48,192]{2,0,1:T(8,128)(2,1)}), bf16[16,1536,192]{2,0,1:T(8,128)(2,1)}) %all-gather.2.cloned.1.call-update) | async-done | bytes 9437200 | tf_op jit(solution)/shard_map/all_gather | solution.py:61
  373.0 21.7 %fusion = f32[16,192,192]{2,1,0:T(8,128)S(1)} fusion(bf16[16,1536,192]{2,0,1:T(8,128)(2,1)} %all-gather.2.cloned.1.call-done), kind=kOutput, calls=%fused_computation.1 | convolution fusion | flops 1811939328 | bytes 11796480 | tf_op jit(solution)/shard_map/nrk,nrl->nkl/dot_general | solution.py:44
  394.7 0.0 copy-done
  394.7 3.6 add_convert_fusion.2
  398.3 17.7 %add_convert_fusion = bf16[16,1536,192]{2,1,0:T(8,128)(2,1)} fusion(bf16[16,192,192]{2,1,0:T(8,128)(2,1)S(1)} %add_convert_fusion.2, bf16[16,1536,192]{2,0,1:T(8,128)(2,1)} %all-gather.2.cloned.1.call-done), kind=kOutput, calls=%fused_computation | convolution fusion | flops 1830813696 | bytes 20054016 | tf_op jit(solution)/shard_map/nrk,nkl->nrl/dot_general | solution.py:52
  416.0 11.3 %fusion.15 = f32[16,192,192]{2,1,0:T(8,128)S(1)} fusion(bf16[16,1536,192]{2,1,0:T(8,128)(2,1)} %add_convert_fusion), kind=kOutput, calls=%fused_computation.44 | convolution fusion | flops 1811939328 | bytes 11796480 | tf_op jit(solution)/shard_map/nrk,nrl->nkl/dot_general | solution.py:44
  427.4 3.5 add_convert_fusion.1
  430.8 0.0 copy-start.2
  430.9 16.4 %fusion.16 = f32[16,1536,192]{2,1,0:T(8,128)} fusion(bf16[16,1536,192]{2,1,0:T(8,128)(2,1)} %add_convert_fusion, bf16[16,192,192]{2,1,0:T(8,128)(2,1)S(1)} %add_convert_fusion.1), kind=kOutput, calls=%fused_computation.45 | convolution fusion | flops 1811939328 | bytes 29491200 | tf_op jit(solution)/shard_map/nrk,nkl->nrl/dot_general | solution.py:52
  447.2 0.0 copy-done.2
  447.2 2.4 multiply_select_fusion
  (8 shorter events, 0.0 us)
Async XLA Ops:
  7.2 192.8 %reduce-scatter.2.cloned.1.call-start = ((), (), s32[]{:S(2)}) async-start(), calls=%async_computation.2 | async-start | bytes 12976128 | tf_op jit(solution)/shard_map/reduce_scatter | solution.py:78
  23.8 0.7 copy-start.4
  23.9 187.7 %copy-start.5 = (f32[1,64]{1,0:T(1,128)S(1)}, f32[1,64]{1,0:T(1,128)}, u32[]{:S(2)}) copy-start(f32[1,64]{1,0:T(1,128)} %param.11) | copy-start | bytes 772
  23.9 207.6 %copy-start.1 = (f32[16,48,192]{2,1,0:T(8,128)S(1)}, f32[16,48,192]{2,1,0:T(8,128)}, u32[]{:S(2)}) copy-start(f32[16,48,192]{2,1,0:T(8,128)} %param.8) | copy-start | bytes 1769476
  202.9 96.3 %copy-start.3 = (f32[8,16,128]{2,1,0:T(8,128)S(1)}, f32[8,16,128]{2,1,0:T(8,128)}, u32[]{:S(2)}) copy-start(f32[8,16,128]{2,1,0:T(8,128)} %param.10) | copy-start | bytes 196612
  202.9 28.6 %all-to-all-start = ((f32[16,48,192]{2,1,0:T(8,128)}), f32[16,48,192]{2,1,0:T(8,128)S(1)}, u32[]{:S(2)}, u32[]{:S(2)}) async-start(f32[16,48,192]{2,1,0:T(8,128)} %copy.58), calls=%async_computation.1 | async-start | bytes 1572864 | tf_op jit(solution)/shard_map/all_to_all | solution.py:92
  211.5 161.5 %all-gather.2.cloned.1.call-start = ((), (), s32[]{:S(2)}) async-start(), calls=%async_computation.3 | async-start | bytes 12976128 | tf_op jit(solution)/shard_map/all_gather | solution.py:61
  231.7 163.0 %copy-start = (f32[16,48,192]{2,1,0:T(8,128)}, f32[16,48,192]{2,1,0:T(8,128)S(1)}, u32[]{:S(2)}) copy-start(f32[16,48,192]{2,1,0:T(8,128)S(1)} %get-tuple-element.17) | copy-start | bytes 1769476
  430.8 16.4 %copy-start.2 = (f32[16,48,192]{2,1,0:T(8,128)S(1)}, f32[16,48,192]{2,1,0:T(8,128)}, u32[]{:S(2)}) copy-start(f32[16,48,192]{2,1,0:T(8,128)} %param.9) | copy-start | bytes 1769476
Sparse Core Ops, SparseCore 0:
  24.0 175.8 reduce-scatter.1
  299.1 73.8 all-gather.1
where the time goes:
time: 457 us; the launch traced here: 456 us
  waiting for transfers between devices  257 us (56%)
  blocking collectives  77 us (17%)
  matrix products  75.8 us (17%)
  between operations  14.2 us (3%)
  local copies, waits for them, and re-layouts  12.1 us (3%)
  other arithmetic  11.5 us (3%)
  starting transfers between devices  8.69 us (2%)
    reduce_scatter x1, waiting for transfers between devices, body(): lax.psum_scatter(partial_value.astype(jnp.float32), ('dp', 'context'), sc...  175 us
    all_gather x1, waiting for transfers between devices, orthogonalize(): gathered = lax.all_gather(iterate, ('dp', 'context'), axis=1, tiled=True)  73.1 us
    psum x1, blocking collectives, orthogonalize(): lax.psum(jnp.sum(matrix * matrix, axis=(1, 2)), ('dp', 'context'))  66.2 us
    dot_general x2, matrix products, quintic(): jnp.einsum('nrk,nkl->nrl', whole, polynomial, preferred_element_type=jnp....  34.1 us
    dot_general x2, matrix products, quintic(): jnp.einsum('nrk,nrl->nkl', whole, whole, preferred_element_type=jnp.float32)  33.1 us
    pmax x1, blocking collectives, body(): peak_logit = lax.pmax(max_logits[0], 'context')  10.9 us
    unnamed x13, local copies, waits for them, and re-layouts  9.79 us
  transfers between devices with their start and end apart: 3, of which 3 were waited for; matrix products, arithmetic and copies ran while one was open for 0% of the time, Pallas kernels for 0%

commit v1 on v0

--- a/solution.py
+++ b/solution.py
@@ -55,7 +55,11 @@
 
 
 def orthogonalize(matrix):
-    square_sum = lax.psum(jnp.sum(matrix * matrix, axis=(1, 2)), ("dp", "context"))
+
+    def drive_unit(a0):
+        return jnp.sum(lax.all_gather(a0, ("dp", "context")), 0)
+
+    square_sum = drive_unit(jnp.sum(matrix * matrix, axis=(1, 2)))
     iterate = (matrix / (jnp.sqrt(square_sum) + 1e-07)[:, None, None]).astype(jnp.bfloat16)
     row_count = matrix.shape[1]
     gathered = lax.all_gather(iterate, ("dp", "context"), axis=1, tiled=True)

time: 457 us -> 458 us (level)
    unnamed x0 -> x1, blocking collectives: none -> 66.3 us
    psum x1 -> x0, blocking collectives: 66.2 us -> none  [orthogonalize(): lax.psum(jnp.sum(matrix * matrix, axis=(1, 2)), ('dp', 'context'))]
    unnamed x13 -> x18, local copies, waits for them, and re-layouts: 9.79 us -> 10.6 us
where the time goes in v1:
time: 458 us; the launch traced here: 457 us
  waiting for transfers between devices  256 us (56%)
  blocking collectives  77.2 us (17%)
  matrix products  75.9 us (17%)
  between operations  14.8 us (3%)
  local copies, waits for them, and re-layouts  13 us (3%)
  other arithmetic  11.5 us (3%)
  starting transfers between devices  8.69 us (2%)
    reduce_scatter x1, waiting for transfers between devices, body(): lax.psum_scatter(partial_value.astype(jnp.float32), ('dp', 'context'), sc...  175 us
    all_gather x1, waiting for transfers between devices, orthogonalize(): gathered = lax.all_gather(iterate, ('dp', 'context'), axis=1, tiled=True)  73.1 us
    unnamed x1, blocking collectives  66.3 us
    dot_general x2, matrix products, quintic(): jnp.einsum('nrk,nkl->nrl', whole, polynomial, preferred_element_type=jnp....  34.1 us
    dot_general x2, matrix products, quintic(): jnp.einsum('nrk,nrl->nkl', whole, whole, preferred_element_type=jnp.float32)  33.2 us
    pmax x1, blocking collectives, body(): peak_logit = lax.pmax(max_logits[0], 'context')  10.9 us
    unnamed x18, local copies, waits for them, and re-layouts  10.6 us
  transfers between devices with their start and end apart: 3, of which 3 were waited for; matrix products, arithmetic and copies ran while one was open for 0% of the time, Pallas kernels for 0%

profile of v1, /device:TPU:1, one launch (start us, length us, event | category | flops | bytes accessed | tf_op | source)
XLA Modules:
  0.0 457.0 jit_solution(2884689237215560987)
XLA Ops:
  7.2 0.0 reduce-scatter.2.cloned.1.call-start
  7.2 9.2 %copy.73 = bf16[1,1536,8,192]{3,2,1,0:T(8,128)(2,1)} copy(bf16[1,1536,8,192]{1,3,2,0:T(8,128)(2,1)} %param.6) | data formatting | bytes 9437184 | tf_op args[0]
  16.4 7.5 %bitcast_convert_fusion = f32[1536,8,192]{2,1,0:T(8,128)} fusion(bf16[1,1536,8,192]{3,2,1,0:T(8,128)(2,1)} %copy.73), kind=kLoop, calls=%fused_computation.4 | loop fusion | flops 2359296 | bytes 14155776 | tf_op jit(solution)/shard_map/convert_element_type | solution.py:83
  23.8 0.0 copy-start.4
  23.8 0.0 reduce-scatter.2.cloned.1.call-update
  23.9 0.0 copy-start.6
  23.9 0.0 copy-start.5
  23.9 0.0 copy-start.1
  23.9 0.6 copy-done.4
  24.5 0.2 convert_reduce_fusion
  24.7 0.1 fusion.13
  24.7 175.2 %reduce-scatter.2.cloned.1.call-done = f32[48,8,192]{2,1,0:T(8,128)} async-done(((f32[1536,8,192]{2,1,0:T(8,128)}), f32[48,8,192]{2,1,0:T(8,128)}) %reduce-scatter.2.cloned.1.call-update) | async-done | bytes 294928 | tf_op jit(solution)/shard_map/reduce_scatter | solution.py:82
  199.9 1.6 fusion.8
  201.5 1.3 copy.74
  202.9 0.0 copy-start.3
  202.9 8.6 %all-to-all-start = ((f32[16,48,192]{2,1,0:T(8,128)}), f32[16,48,192]{2,1,0:T(8,128)S(1)}, u32[]{:S(2)}, u32[]{:S(2)}) async-start(f32[16,48,192]{2,1,0:T(8,128)} %copy.74), calls=%async_computation.1 | async-start | bytes 1572864 | tf_op jit(solution)/shard_map/all_to_all | solution.py:96
  211.5 0.0 all-gather.3.cloned.1.call-start
  211.5 0.0 copy-done.6
  211.5 0.6 dynamic-slice.1
  212.8 0.0 copy-done.5
  212.8 10.9 %pmax.7 = f32[64]{0:T(128)S(1)} all-reduce(f32[64]{0:T(128)S(1)} %bitcast.25), channel_id=1, replica_groups=mesh['dp'=8,'owner'=8,'context'=4] {'context'}, use_global_device_ids=true, to_apply=%region_5.6 | all-reduce | flops 64 | bytes 512 | tf_op jit(solution)/shard_map/pmax | solution.py:79
  223.7 0.1 select_reduce_fusion
  223.8 7.6 %all-to-all-done = f32[16,48,192]{2,1,0:T(8,128)S(1)} async-done(((f32[16,48,192]{2,1,0:T(8,128)}), f32[16,48,192]{2,1,0:T(8,128)S(1)}, u32[]{:S(2)}, u32[]{:S(2)}) %all-to-all-start) | async-done | bytes 589856 | tf_op jit(solution)/shard_map/all_to_all | solution.py:96
  231.4 0.0 copy-done.1
  231.4 0.3 multiply_reduce_fusion
  231.7 0.0 copy-start
  231.8 0.2 dynamic-update-slice
  232.0 66.3 %all-reduce = f32[512]{0:T(512)S(1)} all-reduce(f32[512]{0:T(512)S(1)} %dynamic-update-slice), channel_id=2, replica_groups=mesh['dp'=8,'owner'=8,'context'=4] {'dp','context'}, use_global_device_ids=true, to_apply=%add | all-reduce | flops 512 | bytes 4096
  298.3 0.1 reshape.112
  298.4 0.1 divide_convert_fusion
  298.6 0.9 copy.75
  299.5 0.0 all-gather.3.cloned.1.call-update
  299.5 0.1 dynamic-slice_sqrt_fusion
  299.6 0.1 broadcast_select_fusion
  299.7 0.0 copy-done.3
  299.7 0.7 broadcast_multiply_fusion
  300.4 73.1 %all-gather.3.cloned.1.call-done = bf16[16,1536,192]{2,0,1:T(8,128)(2,1)} async-done(((bf16[16,48,192]{2,0,1:T(8,128)(2,1)}), bf16[16,1536,192]{2,0,1:T(8,128)(2,1)}) %all-gather.3.cloned.1.call-update) | async-done | bytes 9437200 | tf_op jit(solution)/shard_map/all_gather | solution.py:65
  373.5 21.8 %fusion = f32[16,192,192]{2,1,0:T(8,128)S(1)} fusion(bf16[16,1536,192]{2,0,1:T(8,128)(2,1)} %all-gather.3.cloned.1.call-done), kind=kOutput, calls=%fused_computation.1 | convolution fusion | flops 1811939328 | bytes 11796480 | tf_op jit(solution)/shard_map/nrk,nrl->nkl/dot_general | solution.py:44
  395.3 0.0 copy-done
  395.3 3.6 add_convert_fusion.2
  398.9 17.7 %add_convert_fusion = bf16[16,1536,192]{2,1,0:T(8,128)(2,1)} fusion(bf16[16,192,192]{2,1,0:T(8,128)(2,1)S(1)} %add_convert_fusion.2, bf16[16,1536,192]{2,0,1:T(8,128)(2,1)} %all-gather.3.cloned.1.call-done), kind=kOutput, calls=%fused_computation | convolution fusion | flops 1830813696 | bytes 20054016 | tf_op jit(solution)/shard_map/nrk,nkl->nrl/dot_general | solution.py:52
  416.6 11.4 %fusion.15 = f32[16,192,192]{2,1,0:T(8,128)S(1)} fusion(bf16[16,1536,192]{2,1,0:T(8,128)(2,1)} %add_convert_fusion), kind=kOutput, calls=%fused_computation.44 | convolution fusion | flops 1811939328 | bytes 11796480 | tf_op jit(solution)/shard_map/nrk,nrl->nkl/dot_general | solution.py:44
  428.0 3.5 add_convert_fusion.1
  431.4 0.0 copy-start.2
  431.5 16.4 %fusion.16 = f32[16,1536,192]{2,1,0:T(8,128)} fusion(bf16[16,1536,192]{2,1,0:T(8,128)(2,1)} %add_convert_fusion, bf16[16,192,192]{2,1,0:T(8,128)(2,1)S(1)} %add_convert_fusion.1), kind=kOutput, calls=%fused_computation.45 | convolution fusion | flops 1811939328 | bytes 29491200 | tf_op jit(solution)/shard_map/nrk,nkl->nrl/dot_general | solution.py:52
  447.8 0.0 copy-done.2
  447.8 2.4 multiply_select_fusion
  (10 shorter events, 0.1 us)
Async XLA Ops:
  7.2 192.8 %reduce-scatter.2.cloned.1.call-start = ((), (), s32[]{:S(2)}) async-start(), calls=%async_computation.2 | async-start | bytes 12976128 | tf_op jit(solution)/shard_map/reduce_scatter | solution.py:82
  23.8 0.7 copy-start.4
  23.9 187.7 %copy-start.6 = (u32[256]{0:T(256)S(1)}, u32[256]{0:T(256)}, u32[]{:S(2)}) copy-start(u32[256]{0:T(256)} %constant.82) | copy-start | bytes 3076
  23.9 188.9 %copy-start.5 = (f32[1,64]{1,0:T(1,128)S(1)}, f32[1,64]{1,0:T(1,128)}, u32[]{:S(2)}) copy-start(f32[1,64]{1,0:T(1,128)} %param.11) | copy-start | bytes 772
  23.9 207.5 %copy-start.1 = (f32[16,48,192]{2,1,0:T(8,128)S(1)}, f32[16,48,192]{2,1,0:T(8,128)}, u32[]{:S(2)}) copy-start(f32[16,48,192]{2,1,0:T(8,128)} %param.8) | copy-start | bytes 1769476
  202.9 96.8 %copy-start.3 = (f32[8,16,128]{2,1,0:T(8,128)S(1)}, f32[8,16,128]{2,1,0:T(8,128)}, u32[]{:S(2)}) copy-start(f32[8,16,128]{2,1,0:T(8,128)} %param.10) | copy-start | bytes 196612
  202.9 28.6 %all-to-all-start = ((f32[16,48,192]{2,1,0:T(8,128)}), f32[16,48,192]{2,1,0:T(8,128)S(1)}, u32[]{:S(2)}, u32[]{:S(2)}) async-start(f32[16,48,192]{2,1,0:T(8,128)} %copy.74), calls=%async_computation.1 | async-start | bytes 1572864 | tf_op jit(solution)/shard_map/all_to_all | solution.py:96
  211.5 162.0 %all-gather.3.cloned.1.call-start = ((), (), s32[]{:S(2)}) async-start(), calls=%async_computation.3 | async-start | bytes 12976128 | tf_op jit(solution)/shard_map/all_gather | solution.py:65
  231.7 163.5 %copy-start = (f32[16,48,192]{2,1,0:T(8,128)}, f32[16,48,192]{2,1,0:T(8,128)S(1)}, u32[]{:S(2)}) copy-start(f32[16,48,192]{2,1,0:T(8,128)S(1)} %get-tuple-element.20) | copy-start | bytes 1769476
  431.4 16.4 %copy-start.2 = (f32[16,48,192]{2,1,0:T(8,128)S(1)}, f32[16,48,192]{2,1,0:T(8,128)}, u32[]{:S(2)}) copy-start(f32[16,48,192]{2,1,0:T(8,128)} %param.9) | copy-start | bytes 1769476
Sparse Core Ops, SparseCore 0:
  24.0 175.8 reduce-scatter.1
  299.6 73.8 all-gather.2
